TPU v7x, 256 devices: a whole 4x4x8 slice. The times are simulated.
256 devices in a mesh: ctx: 2 (over core), head: 4 (over x), doc: 32 (over z, y).
Axes of the slice: x: 4, y: 4, z: 8, core: 2. Of those that a mesh axis runs over, the one named last changes fastest.
Arguments:
- queries: bfloat16 [32, 256, 8192], P('doc', 'ctx', 'head'), may hold values from -360 to 360
- keys: bfloat16 [32, 8192, 1024], P('doc', 'ctx', 'head'), may hold values from -6 to 6
- values: bfloat16 [32, 8192, 1024], P('doc', 'ctx', 'head'), may hold values from -6 to 6
- pattern: int32 [32, 2, 16], P('doc'), may hold values from 0 to 63, as said below
Outputs:
- attended: bfloat16 [32, 256, 8192], P('doc', 'ctx', 'head')
- gram: float32 [8192, 8192], P(('head', 'ctx'), 'doc')
Inputs may be any that keep to these rules, and one draw needn't show every extreme that they name: Each row pattern[d, b, :] lists 16 different block numbers; no context shard (blocks s * 32 to (s + 1) * 32 - 1) holds more than 12 of one row's blocks, and in every draw some row has exactly 12 of its blocks in one shard.
All inputs are finite; a program needn't handle non-finite values.
Results may differ from a plain program's by a relative error of at most 0.015.
Values may be sent and summed in bfloat16 or wider, within the bound.
No kernel may reach another device: no remote copies, remote signals or barrier semaphores. Data moves between devices by JAX's collectives and lax.ppermute only.
A program may use at most 128 MiB of HBM per device.

v0:
```python
import jax
import jax.numpy as jnp
from jax import lax
from jax.sharding import PartitionSpec as P

HEAD_SIZE = 128
BLOCK_TOKENS = 128
QB_DEV = 1
NKB_DEV = 32
GROUP = 8
CAP = 12
NEGATIVE = -1e30


def in_order(pieces, dim):
    pieces = jnp.moveaxis(pieces, 0, dim)
    lengths = pieces.shape
    return pieces.reshape(*lengths[:dim], lengths[dim] * lengths[dim + 1], *lengths[dim + 2 :])


def sent_to_all(value, axis):
    size = lax.axis_size(axis)
    return lax.all_to_all(
        jnp.broadcast_to(value[None], (size, *value.shape)), axis, 0, 0, tiled=True
    )


def collect(value, axis, dim):
    return in_order(sent_to_all(value, axis), dim)


def in_blocks(value, dim, size):
    lengths = value.shape
    pieces = value.reshape(*lengths[:dim], size, lengths[dim] // size, *lengths[dim + 1 :])
    return jnp.moveaxis(pieces, dim, 0)


def cut_rows(length, count):
    lap = length // count
    if lap >= 8:
        lap -= lap % 8
    return [lap * k for k in range(1, count)]


def several_exchanges(value, axis, pieces, split_dim, concat_dim):
    blocks = in_blocks(value, split_dim, lax.axis_size(axis))
    split_at = max(range(1, max(2, blocks.ndim - 1)), key=lambda d: blocks.shape[d])
    gathered = []
    for share in jnp.split(blocks, cut_rows(blocks.shape[split_at], pieces), axis=split_at):
        if share.size:
            gathered.append(lax.all_to_all(share, axis, split_axis=0, concat_axis=0, tiled=True))
    return in_order(jnp.concatenate(gathered, axis=split_at), concat_dim)


def owned_slots(pattern_rows, owner):
    mine = pattern_rows // NKB_DEV == owner
    order = jnp.argsort(1 - mine.astype(jnp.int32), axis=1, stable=True)[:, :CAP]
    picked = jnp.take_along_axis(pattern_rows, order, axis=1) % NKB_DEV
    valid = jnp.take_along_axis(mine, order, axis=1)
    return (picked, valid)


def attend_block(query, key_blocks, value_blocks, valid):
    slots = key_blocks.shape[0]
    kv_heads = key_blocks.shape[2] // HEAD_SIZE
    grouped = query.reshape(BLOCK_TOKENS, kv_heads, GROUP, HEAD_SIZE)
    key_row_list = key_blocks.reshape(slots * BLOCK_TOKENS, kv_heads, HEAD_SIZE)
    value_row_list = value_blocks.reshape(slots * BLOCK_TOKENS, kv_heads, HEAD_SIZE)
    scores = jnp.einsum(
        "qkgd,skd->kgqs", grouped, key_row_list, preferred_element_type=jnp.float32
    ) * HEAD_SIZE ** (-0.5)
    live = jnp.broadcast_to(valid[:, None], (slots, BLOCK_TOKENS)).reshape(slots * BLOCK_TOKENS)
    scores = jnp.where(live, scores, NEGATIVE)
    top = jnp.max(scores, axis=-1)
    weights = jnp.where(live, jnp.exp(scores - top[..., None]), 0.0)
    total = jnp.sum(weights, axis=-1)
    mixed = jnp.einsum(
        "kgqs,skd->qkgd",
        weights.astype(jnp.bfloat16),
        value_row_list,
        preferred_element_type=jnp.float32,
    )
    heads = kv_heads * GROUP
    top_rows = jnp.transpose(top, (2, 0, 1)).reshape(BLOCK_TOKENS, heads)
    total_rows = jnp.transpose(total, (2, 0, 1)).reshape(BLOCK_TOKENS, heads)
    return (mixed.reshape(BLOCK_TOKENS, heads, HEAD_SIZE), top_rows, total_rows)


def per_device(queries, keys, values, pattern):
    ctx_count = lax.axis_size("ctx")
    head_count = lax.axis_size("head")
    doc_count = lax.axis_size("doc")
    owner = lax.axis_index("ctx")
    tok_rows = queries.shape[1]
    width = queries.shape[2]
    key_blocks = keys[0].reshape(NKB_DEV, BLOCK_TOKENS, keys.shape[2])
    value_blocks = values[0].reshape(NKB_DEV, BLOCK_TOKENS, values.shape[2])
    picked, valid = owned_slots(pattern[0], owner)
    send_keys = key_blocks[picked].reshape(ctx_count, QB_DEV, CAP, BLOCK_TOKENS, keys.shape[2])
    send_values = value_blocks[picked].reshape(
        ctx_count, QB_DEV, CAP, BLOCK_TOKENS, values.shape[2]
    )
    got_keys, got_values = (
        lax.all_to_all(send_keys, "ctx", split_axis=0, concat_axis=0, tiled=True),
        lax.all_to_all(send_values, "ctx", split_axis=0, concat_axis=0, tiled=True),
    )
    got_keys = jnp.swapaxes(got_keys, 0, 1).reshape(
        QB_DEV, ctx_count * CAP, BLOCK_TOKENS, keys.shape[2]
    )
    got_values = jnp.swapaxes(got_values, 0, 1).reshape(
        QB_DEV, ctx_count * CAP, BLOCK_TOKENS, values.shape[2]
    )
    own_rows = lax.dynamic_slice_in_dim(pattern[0], owner * QB_DEV, QB_DEV, 0)
    sources = jnp.arange(ctx_count, dtype=jnp.int32)
    counts = jnp.sum(own_rows[:, :, None] // NKB_DEV == sources[None, None, :], axis=1)
    live = (jnp.arange(CAP)[None, None, :] < counts[:, :, None]).reshape(QB_DEV, ctx_count * CAP)
    query_block_list = queries[0].reshape(QB_DEV, BLOCK_TOKENS, width)

    def one_owned(items):
        query, key_set, value_set, ok = items
        return attend_block(query, key_set, value_set, ok)

    mixed, top, total = lax.map(one_owned, (query_block_list, got_keys, got_values, live))
    attended = (mixed / total[..., None]).astype(jnp.bfloat16).reshape(tok_rows, width)
    sub = width // ctx_count
    model_width = width * head_count
    span = collect(attended, "ctx", 0)
    mine_cols = lax.dynamic_slice_in_dim(span, owner * sub, sub, 1)
    full_doc = lax.all_gather(span, "head", axis=1, tiled=True)
    slice_width = model_width // doc_count
    split_cols = full_doc.reshape(tok_rows * ctx_count, doc_count, slice_width)
    column_set = several_exchanges(split_cols, "doc", 2, 1, 0).reshape(
        doc_count * tok_rows * ctx_count, slice_width
    )
    product = lax.dot_general(
        lax.all_gather(mine_cols, "doc", axis=0, tiled=True),
        column_set,
        (((0,), (0,)), ((), ())),
        preferred_element_type=jnp.float32,
    )
    return (attended.reshape(1, tok_rows, width), product)


def solution(mesh):
    placed = (
        P("doc", "ctx", "head"),
        P("doc", "ctx", "head"),
        P("doc", "ctx", "head"),
        P("doc", None, None),
    )
    return jax.shard_map(
        per_device,
        mesh=mesh,
        in_specs=placed,
        out_specs=(P("doc", "ctx", "head"), P(("head", "ctx"), "doc")),
        check_vma=False,
    )
```

profile of v0, /device:TPU:8, one launch (start us, length us, event | category | flops | bytes accessed | tf_op | source)
XLA Modules:
  0.0 352.8 jit_solution(10864204959958701672)
XLA Ops:
  7.2 0.9 copy.62
  8.1 0.7 sort.17
  9.0 1.5 gather_fusion.2
  10.6 0.1 copy.67
  10.9 1.9 gather_fusion.1
  12.8 3.8 %all-to-all-start.1 = ((bf16[2,1,12,128,256]{4,3,2,1,0:T(8,128)(2,1)}), bf16[2,1,12,128,256]{4,3,2,1,0:T(8,128)(2,1)S(1)}, u32[]{:S(2)}, u32[]{:S(2)}) async-start(bf16[2,1,12,128,256]{4,3,2,1,0:T(8,128)(2,1)} %bitcast.79), calls=%async_computation.1 | async-start | bytes 3145728 | tf_op jit(solution)/shard_map/all_to_all | solution.py:104
  16.6 0.1 fusion.30
  17.1 0.1 copy.91
  17.2 3.4 gather_fusion
  20.7 4.7 %all-to-all-start = ((bf16[2,1,12,128,256]{4,3,2,1,0:T(8,128)(2,1)}), bf16[2,1,12,128,256]{4,3,2,1,0:T(8,128)(2,1)}, u32[]{:S(2)}, u32[]{:S(2)}) async-start(bf16[2,1,12,128,256]{4,3,2,1,0:T(8,128)(2,1)} %bitcast.80), calls=%async_computation | async-start | bytes 3145728 | tf_op jit(solution)/shard_map/all_to_all | solution.py:105
  25.4 1.9 reshape.226
  27.2 17.6 %fusion.33 = (f32[2,8,128]{2,1,0:T(8,128)S(1)}, bf16[2,8,128,3072]{2,3,1,0:T(8,128)(2,1)}) fusion(pred[3072]{0:T(1024)(128)(4,1)S(1)} %broadcast_bitcast_fusion, bf16[3072,2,128,1]{2,1,0,3:T(2,128)(2,1)} %bitcast.84, bf16[128,2,8,128]{3,2,1,0:T(8,128)(2,1)S(1)} %bitcast.87), kind=kOutput, calls=%fused_computation.58 | convolution fusion | flops 1648364544 | bytes 14691328 | tf_op jit(solution)/shard_map/while/body/eval_jaxpr/sub | solution.py:75
  44.8 3.5 reshape.223
  48.3 7.0 %fusion.6 = f32[2,128,8,128]{3,1,2,0:T(8,128)S(1)} fusion(bf16[2,8,128,3072]{2,3,1,0:T(8,128)(2,1)} %get-tuple-element.28, bf16[3072,2,128,1]{2,1,0,3:T(2,128)(2,1)} %bitcast.81), kind=kOutput, calls=%fused_computation.10 | convolution fusion | flops 1610612736 | bytes 15204352 | tf_op jit(solution)/shard_map/while/body/eval_jaxpr/kgqs,skd->qkgd/dot_general | solution.py:77
  55.5 4.6 %all_to_all.25 = bf16[2,128,2048]{1,2,0:T(8,128)(2,1)S(1)} all-to-all(bf16[2,128,2048]{1,2,0:T(8,128)(2,1)S(1)} %broadcast_in_dim.63), channel_id=1, replica_groups=mesh['ctx'=2,'head'=4,'doc'=32] {'ctx'}, dimensions={0} | all-to-all | bytes 2097152 | tf_op jit(solution)/shard_map/all_to_all | solution.py:23
  60.0 1.1 copy_bitcast_fusion
  61.2 1.9 constant_dynamic-slice_fusion
  63.1 51.9 %all-gather.5.cloned.1.call-done = bf16[256,8192]{0,1:T(8,128)(2,1)} async-done(((bf16[256,2048]{0,1:T(8,128)(2,1)}), bf16[256,8192]{0,1:T(8,128)(2,1)}) %all-gather.5.cloned.1.call-update) | async-done | bytes 4194320 | tf_op jit(solution)/shard_map/all_gather | solution.py:129
  115.0 4.0 %slice_bitcast_fusion.1 = (bf16[32,128,1,256]{1,3,2,0:T(8,128)(2,1)S(1)}, bf16[32,128,1,256]{1,3,2,0:T(8,128)(2,1)}) fusion(bf16[32,256,1,256]{1,3,0,2:T(8,128)(2,1)} %bitcast.82), kind=kLoop, calls=%fused_computation.18 | loop fusion | bytes 8388608 | tf_op jit(solution)/shard_map/split | solution.py:49
  119.0 74.1 %all_to_all.26 = bf16[32,128,1,256]{1,3,2,0:T(8,128)(2,1)} all-to-all(bf16[32,128,1,256]{1,3,2,0:T(8,128)(2,1)S(1)} %get-tuple-element.18), channel_id=1, replica_groups=mesh['ctx'=2,'head'=4,'doc'=32] {'doc'}, dimensions={0} | all-to-all | bytes 4194304 | tf_op jit(solution)/shard_map/all_to_all | solution.py:51
  193.1 5.7 %all-to-all-start.4 = ((bf16[32,128,1,256]{1,3,2,0:T(8,128)(2,1)}), bf16[32,128,1,256]{1,3,2,0:T(8,128)(2,1)}, u32[]{:S(2)}, u32[]{:S(2)}) async-start(bf16[32,128,1,256]{1,3,2,0:T(8,128)(2,1)} %get-tuple-element.19), calls=%async_computation.4 | async-start | bytes 4194304 | tf_op jit(solution)/shard_map/all_to_all | solution.py:51
  198.8 0.1 copy.74
  198.9 0.3 copy.75
  199.2 1.3 div.59
  200.5 2.5 div.60
  203.1 2.2 divide_convert_fusion
  205.2 2.9 copy.80
  208.2 51.0 %all-to-all-done.4 = bf16[32,128,1,256]{1,3,2,0:T(8,128)(2,1)} async-done(((bf16[32,128,1,256]{1,3,2,0:T(8,128)(2,1)}), bf16[32,128,1,256]{1,3,2,0:T(8,128)(2,1)}, u32[]{:S(2)}, u32[]{:S(2)}) %all-to-all-start.4) | async-done | bytes 2097184 | tf_op jit(solution)/shard_map/all_to_all | solution.py:51
  259.2 4.1 %copy.81 = bf16[32,128,1,256]{3,1,0,2:T(8,128)(2,1)} copy(bf16[32,128,1,256]{1,3,2,0:T(8,128)(2,1)} %all-to-all-done.4) | data formatting | bytes 4194304 | tf_op jit(solution)/shard_map/all_to_all | solution.py:51
  263.3 4.0 %pad_maximum_fusion = bf16[32,256,1,256]{3,1,0,2:T(8,128)(2,1)} fusion(bf16[32,128,1,256]{3,1,0,2:T(8,128)(2,1)} %copy.81, bf16[32,128,1,256]{3,1,0,2:T(8,128)(2,1)S(1)} %copy-done.4), kind=kLoop, calls=%fused_computation.15 | loop fusion | flops 8388608 | bytes 8388608 | tf_op jit(solution)/shard_map/concatenate | solution.py:52
  267.3 66.1 %all-gather.3.cloned.1.call-done = bf16[8192,1024]{0,1:T(8,128)(2,1)} async-done(((bf16[256,1024]{0,1:T(8,128)(2,1)}), bf16[8192,1024]{0,1:T(8,128)(2,1)}) %all-gather.3.cloned.1.call-update) | async-done | bytes 16777232 | tf_op jit(solution)/shard_map/all_gather | solution.py:136
  333.3 12.6 %fusion.42 = f32[1024,256]{1,0:T(8,128)} fusion(bf16[8192,1024]{0,1:T(8,128)(2,1)} %all-gather.3.cloned.1.call-done, bf16[8192,256]{1,0:T(8,128)(2,1)} %bitcast.83), kind=kOutput, calls=%fused_computation.59 | convolution fusion | flops 4294967296 | bytes 22020096 | tf_op jit(solution)/shard_map/dot_general | solution.py:135
  (38 shorter events, 1.2 us)
Async XLA Ops:
  7.2 3.8 %copy-start = (bf16[1,4096,256]{2,1,0:T(8,128)(2,1)S(1)}, bf16[1,4096,256]{2,1,0:T(8,128)(2,1)}, u32[]{:S(2)}) copy-start(bf16[1,4096,256]{2,1,0:T(8,128)(2,1)} %param.5) | copy-start | bytes 6291460
  12.8 3.8 %copy-start.2 = (s32[1,2,16]{2,1,0:T(2,128)S(1)}, s32[1,2,16]{2,1,0:T(2,128)}, u32[]{:S(2)}) copy-start(s32[1,2,16]{2,1,0:T(2,128)} %param.7) | copy-start | bytes 388
  12.8 4.3 %copy-start.5 = (bf16[1,128,2048]{2,1,0:T(8,128)(2,1)S(1)}, bf16[1,128,2048]{2,1,0:T(8,128)(2,1)}, u32[]{:S(2)}) copy-start(bf16[1,128,2048]{2,1,0:T(8,128)(2,1)} %param.4) | copy-start | bytes 1572868
  12.8 7.9 %all-to-all-start.1 = ((bf16[2,1,12,128,256]{4,3,2,1,0:T(8,128)(2,1)}), bf16[2,1,12,128,256]{4,3,2,1,0:T(8,128)(2,1)S(1)}, u32[]{:S(2)}, u32[]{:S(2)}) async-start(bf16[2,1,12,128,256]{4,3,2,1,0:T(8,128)(2,1)} %bitcast.79), calls=%async_computation.1 | async-start | bytes 3145728 | tf_op jit(solution)/shard_map/all_to_all | solution.py:104
  20.7 24.1 %all-to-all-start = ((bf16[2,1,12,128,256]{4,3,2,1,0:T(8,128)(2,1)}), bf16[2,1,12,128,256]{4,3,2,1,0:T(8,128)(2,1)}, u32[]{:S(2)}, u32[]{:S(2)}) async-start(bf16[2,1,12,128,256]{4,3,2,1,0:T(8,128)(2,1)} %bitcast.80), calls=%async_computation | async-start | bytes 3145728 | tf_op jit(solution)/shard_map/all_to_all | solution.py:105
  25.3 89.7 %all-gather.5.cloned.1.call-start = ((), (), s32[]{:S(2)}) async-start(), calls=%async_computation.6 | async-start | bytes 5242880 | tf_op jit(solution)/shard_map/all_gather | solution.py:129
  61.2 272.2 %all-gather.3.cloned.1.call-start = ((), (), s32[]{:S(2)}) async-start(), calls=%async_computation.5 | async-start | bytes 17301504 | tf_op jit(solution)/shard_map/all_gather | solution.py:136
  193.1 66.0 %all-to-all-start.4 = ((bf16[32,128,1,256]{1,3,2,0:T(8,128)(2,1)}), bf16[32,128,1,256]{1,3,2,0:T(8,128)(2,1)}, u32[]{:S(2)}, u32[]{:S(2)}) async-start(bf16[32,128,1,256]{1,3,2,0:T(8,128)(2,1)} %get-tuple-element.19), calls=%async_computation.4 | async-start | bytes 4194304 | tf_op jit(solution)/shard_map/all_to_all | solution.py:51
  200.5 4.7 %copy-start.3 = (bf16[32,128,1,256]{1,3,2,0:T(8,128)(2,1)S(1)}, bf16[32,128,1,256]{1,3,2,0:T(8,128)(2,1)}, u32[]{:S(2)}) copy-start(bf16[32,128,1,256]{1,3,2,0:T(8,128)(2,1)} %all_to_all.26) | copy-start | bytes 6291460
  208.2 55.1 %copy-start.4 = (bf16[32,128,1,256]{3,1,0,2:T(8,128)(2,1)S(1)}, bf16[32,128,1,256]{3,1,0,2:T(8,128)(2,1)}, u32[]{:S(2)}) copy-start(bf16[32,128,1,256]{3,1,0,2:T(8,128)(2,1)} %copy.80) | copy-start | bytes 6291460
  333.3 12.6 %copy-start.1 = (bf16[1,4096,256]{2,1,0:T(8,128)(2,1)S(1)}, bf16[1,4096,256]{2,1,0:T(8,128)(2,1)}, u32[]{:S(2)}) copy-start(bf16[1,4096,256]{2,1,0:T(8,128)(2,1)} %param.5) | copy-start | bytes 6291460
Sparse Core Ops, SparseCore 0:
  61.3 53.6 all-gather.4
  117.5 215.8 all-gather.2
where the time goes:
time: 353 us
  waiting for transfers between devices  169 us (48%)
  blocking collectives  78.7 us (22%)
  matrix products  37.1 us (11%)
  local copies, waits for them, and re-layouts  32.5 us (9%)
  starting transfers between devices  14.2 us (4%)
  between operations  14.2 us (4%)
  other arithmetic  7.17 us (2%)
    all_to_all x1, blocking collectives, several_exchanges(): lax.all_to_all(share, axis, split_axis=0, concat_axis=0, tiled=True)  74.1 us
    all_gather x1, waiting for transfers between devices, per_device(): lax.all_gather(mine_cols, 'doc', axis=0, tiled=True)  66.1 us
    all_gather x1, waiting for transfers between devices, per_device(): full_doc = lax.all_gather(span, 'head', axis=1, tiled=True)  51.9 us
    all_to_all x1, waiting for transfers between devices, several_exchanges(): lax.all_to_all(share, axis, split_axis=0, concat_axis=0, tiled=True)  51 us
    sub x1, matrix products, attend_block(): weights = jnp.where(live, jnp.exp(scores - top[..., None]), 0.0)  17.6 us
    dot_general x1, matrix products, per_device(): lax.dot_general(lax.all_gather(mine_cols, 'doc', axis=0, tiled=True), col...  12.6 us
  transfers between devices with their start and end apart: 5, of which 3 were waited for; matrix products, arithmetic and copies ran while one was open for 13% of the time, Pallas kernels for 0%

commit v1 on v0

--- a/solution.py
+++ b/solution.py
@@ -1,3 +1,4 @@
+import functools
 import jax
 import jax.numpy as jnp
 from jax import lax
@@ -10,6 +11,21 @@
 GROUP = 8
 CAP = 12
 NEGATIVE = -1e30
+
+
+def compute_the_chunk(slab_in, dev_axis):
+    return jnp.concatenate(
+        lax.all_to_all(
+            jnp.stack([slab_in] * lax.axis_size(dev_axis), axis=0),
+            axis_name=dev_axis,
+            split_axis=0,
+            concat_axis=0,
+        ),
+        axis=0,
+    )
+
+
+_get_keys = functools.partial(compute_the_chunk, dev_axis="doc")
 
 
 def in_order(pieces, dim):
@@ -133,7 +149,7 @@
         doc_count * tok_rows * ctx_count, slice_width
     )
     product = lax.dot_general(
-        lax.all_gather(mine_cols, "doc", axis=0, tiled=True),
+        _get_keys(mine_cols),
         column_set,
         (((0,), (0,)), ((), ())),
         preferred_element_type=jnp.float32,

time: 353 us -> 661 us (1.87)
  the two profiles are of different devices: /device:TPU:8 before, /device:TPU:120 now
where the time goes in v1:
time: 661 us; the launch traced here: 660 us
  waiting for transfers between devices  481 us (73%)
  blocking collectives  62.3 us (9%)
  matrix products  37.1 us (6%)
  local copies, waits for them, and re-layouts  33.7 us (5%)
  starting transfers between devices  25.4 us (4%)
  between operations  14.2 us (2%)
    all_to_all x1, waiting for transfers between devices, compute_the_chunk(): lax.all_to_all(jnp.stack([slab_in] * lax.axis_size(dev_axis), axis=0), ax...  382 us
    all_to_all x1, blocking collectives, several_exchanges(): lax.all_to_all(share, axis, split_axis=0, concat_axis=0, tiled=True)  57.7 us
    all_gather x1, waiting for transfers between devices, per_device(): full_doc = lax.all_gather(span, 'head', axis=1, tiled=True)  52.6 us
    all_to_all x1, waiting for transfers between devices, several_exchanges(): lax.all_to_all(share, axis, split_axis=0, concat_axis=0, tiled=True)  46.2 us
    sub x1, matrix products, attend_block(): weights = jnp.where(live, jnp.exp(scores - top[..., None]), 0.0)  17.6 us
  transfers between devices with their start and end apart: 5, of which 3 were waited for; matrix products, arithmetic and copies ran while one was open for 6% of the time, Pallas kernels for 0%

profile of v1, /device:TPU:120, one launch (start us, length us, event | category | flops | bytes accessed | tf_op | source)
XLA Modules:
  0.0 659.8 jit_solution(3869038775427689752)
XLA Ops:
  7.2 0.9 copy.64
  8.1 0.7 sort.17
  9.0 1.5 gather_fusion.2
  10.9 1.9 gather_fusion.1
  12.8 3.7 all-to-all-start.1
  16.6 0.1 fusion.30
  17.0 0.1 copy.94
  17.1 3.4 gather_fusion
  20.5 4.6 all-to-all-start
  25.2 1.8 reshape.231
  27.1 17.6 %fusion.33 = (f32[2,8,128]{2,1,0:T(8,128)S(1)}, bf16[2,8,128,3072]{2,3,1,0:T(8,128)(2,1)}) fusion(pred[3072]{0:T(1024)(128)(4,1)S(1)} %broadcast_bitcast_fusion, bf16[3072,2,128,1]{2,1,0,3:T(2,128)(2,1)} %bitcast.85, bf16[128,2,8,128]{3,2,1,0:T(8,128)(2,1)S(1)} %bitcast.88), kind=kOutput, calls=%fused_computation.58 | convolution fusion | flops 1648364544 | bytes 14691328 | tf_op jit(solution)/shard_map/while/body/eval_jaxpr/sub | solution.py:91
  44.6 3.5 reshape.228
  48.2 7.0 %fusion.6 = f32[2,128,8,128]{3,1,2,0:T(8,128)S(1)} fusion(bf16[2,8,128,3072]{2,3,1,0:T(8,128)(2,1)} %get-tuple-element.28, bf16[3072,2,128,1]{2,1,0,3:T(2,128)(2,1)} %bitcast.83), kind=kOutput, calls=%fused_computation.10 | convolution fusion | flops 1610612736 | bytes 15204352 | tf_op jit(solution)/shard_map/while/body/eval_jaxpr/kgqs,skd->qkgd/dot_general | solution.py:93
  55.3 4.6 all_to_all.30
  59.9 1.1 copy_bitcast_fusion
  61.0 52.6 %all-gather.2.cloned.1.call-done = bf16[256,8192]{0,1:T(8,128)(2,1)} async-done(((bf16[256,2048]{0,1:T(8,128)(2,1)}), bf16[256,8192]{0,1:T(8,128)(2,1)}) %all-gather.2.cloned.1.call-update) | async-done | bytes 4194320 | tf_op jit(solution)/shard_map/all_gather | solution.py:145
  113.6 4.0 slice_bitcast_fusion.1
  117.6 57.7 %all_to_all.31 = bf16[32,128,1,256]{1,3,2,0:T(8,128)(2,1)} all-to-all(bf16[32,128,1,256]{1,3,2,0:T(8,128)(2,1)S(1)} %get-tuple-element.19), channel_id=1, replica_groups=mesh['ctx'=2,'head'=4,'doc'=32] {'doc'}, dimensions={0} | all-to-all | bytes 4194304 | tf_op jit(solution)/shard_map/all_to_all | solution.py:67
  175.3 8.3 %all-to-all-start.4 = ((bf16[32,128,1,256]{1,3,2,0:T(8,128)(2,1)}), bf16[32,128,1,256]{1,3,2,0:T(8,128)(2,1)}, u32[]{:S(2)}, u32[]{:S(2)}) async-start(bf16[32,128,1,256]{1,3,2,0:T(8,128)(2,1)} %get-tuple-element.18), calls=%async_computation.4 | async-start | bytes 4194304 | tf_op jit(solution)/shard_map/all_to_all | solution.py:67
  183.7 0.2 copy.80
  183.9 46.2 %all-to-all-done.4 = bf16[32,128,1,256]{1,3,2,0:T(8,128)(2,1)} async-done(((bf16[32,128,1,256]{1,3,2,0:T(8,128)(2,1)}), bf16[32,128,1,256]{1,3,2,0:T(8,128)(2,1)}, u32[]{:S(2)}, u32[]{:S(2)}) %all-to-all-start.4) | async-done | bytes 2097184 | tf_op jit(solution)/shard_map/all_to_all | solution.py:67
  230.1 5.9 stack.2
  236.0 8.7 %all-to-all-start.3 = ((bf16[32,256,1024]{2,1,0:T(8,128)(2,1)}), bf16[32,256,1024]{2,1,0:T(8,128)(2,1)}, u32[]{:S(2)}, u32[]{:S(2)}) async-start(bf16[32,256,1024]{2,1,0:T(8,128)(2,1)} %stack.2), calls=%async_computation.3 | async-start | bytes 33554432 | tf_op jit(solution)/shard_map/all_to_all | solution.py:18
  244.8 0.3 copy.77
  245.2 0.3 div.59
  245.5 0.2 div.60
  245.7 0.9 divide_convert_fusion
  246.6 3.3 copy.84
  249.9 4.1 copy.83
  253.9 4.1 pad_maximum_fusion
  258.0 382.3 %all-to-all-done.3 = bf16[32,256,1024]{2,1,0:T(8,128)(2,1)} async-done(((bf16[32,256,1024]{2,1,0:T(8,128)(2,1)}), bf16[32,256,1024]{2,1,0:T(8,128)(2,1)}, u32[]{:S(2)}, u32[]{:S(2)}) %all-to-all-start.3) | async-done | bytes 16777248 | tf_op jit(solution)/shard_map/all_to_all | solution.py:18
  640.4 12.6 %fusion.42 = f32[1024,256]{1,0:T(8,128)} fusion(bf16[8192,1024]{1,0:T(8,128)(2,1)} %bitcast.18, bf16[8192,256]{1,0:T(8,128)(2,1)} %bitcast.79), kind=kOutput, calls=%fused_computation.59 | convolution fusion | flops 4294967296 | bytes 22020096 | tf_op jit(solution)/shard_map/dot_general | solution.py:151
  (37 shorter events, 1.3 us)
Async XLA Ops:
  7.2 3.8 copy-start
  7.2 9.4 %copy-start.2 = (s32[1,2,16]{2,1,0:T(2,128)S(1)}, s32[1,2,16]{2,1,0:T(2,128)}, u32[]{:S(2)}) copy-start(s32[1,2,16]{2,1,0:T(2,128)} %param.7) | copy-start | bytes 388
  7.2 9.8 %copy-start.4 = (bf16[1,128,2048]{2,1,0:T(8,128)(2,1)S(1)}, bf16[1,128,2048]{2,1,0:T(8,128)(2,1)}, u32[]{:S(2)}) copy-start(bf16[1,128,2048]{2,1,0:T(8,128)(2,1)} %param.4) | copy-start | bytes 1572868
  12.8 7.7 %all-to-all-start.1 = ((bf16[2,1,12,128,256]{4,3,2,1,0:T(8,128)(2,1)}), bf16[2,1,12,128,256]{4,3,2,1,0:T(8,128)(2,1)S(1)}, u32[]{:S(2)}, u32[]{:S(2)}) async-start(bf16[2,1,12,128,256]{4,3,2,1,0:T(8,128)(2,1)} %bitcast.81), calls=%async_computation.1 | async-start | bytes 3145728 | tf_op jit(solution)/shard_map/all_to_all | solution.py:120
  20.5 24.1 %all-to-all-start = ((bf16[2,1,12,128,256]{4,3,2,1,0:T(8,128)(2,1)}), bf16[2,1,12,128,256]{4,3,2,1,0:T(8,128)(2,1)}, u32[]{:S(2)}, u32[]{:S(2)}) async-start(bf16[2,1,12,128,256]{4,3,2,1,0:T(8,128)(2,1)} %bitcast.82), calls=%async_computation | async-start | bytes 3145728 | tf_op jit(solution)/shard_map/all_to_all | solution.py:121
  25.2 88.4 %all-gather.2.cloned.1.call-start = ((), (), s32[]{:S(2)}) async-start(), calls=%async_computation.6 | async-start | bytes 5242880 | tf_op jit(solution)/shard_map/all_gather | solution.py:145
  117.6 66.0 %copy-start.3 = (bf16[256,2048]{0,1:T(8,128)(2,1)S(1)}, bf16[256,2048]{0,1:T(8,128)(2,1)}, u32[]{:S(2)}) copy-start(bf16[256,2048]{0,1:T(8,128)(2,1)} %copy_bitcast_fusion) | copy-start | bytes 3145732
  175.3 54.8 %all-to-all-start.4 = ((bf16[32,128,1,256]{1,3,2,0:T(8,128)(2,1)}), bf16[32,128,1,256]{1,3,2,0:T(8,128)(2,1)}, u32[]{:S(2)}, u32[]{:S(2)}) async-start(bf16[32,128,1,256]{1,3,2,0:T(8,128)(2,1)} %get-tuple-element.18), calls=%async_computation.4 | async-start | bytes 4194304 | tf_op jit(solution)/shard_map/all_to_all | solution.py:67
  236.0 404.3 %all-to-all-start.3 = ((bf16[32,256,1024]{2,1,0:T(8,128)(2,1)}), bf16[32,256,1024]{2,1,0:T(8,128)(2,1)}, u32[]{:S(2)}, u32[]{:S(2)}) async-start(bf16[32,256,1024]{2,1,0:T(8,128)(2,1)} %stack.2), calls=%async_computation.3 | async-start | bytes 33554432 | tf_op jit(solution)/shard_map/all_to_all | solution.py:18
  640.3 12.6 %copy-start.1 = (bf16[1,4096,256]{2,1,0:T(8,128)(2,1)S(1)}, bf16[1,4096,256]{2,1,0:T(8,128)(2,1)}, u32[]{:S(2)}) copy-start(bf16[1,4096,256]{2,1,0:T(8,128)(2,1)} %param.5) | copy-start | bytes 6291460
Sparse Core Ops, SparseCore 0:
  61.1 52.4 all-gather.1
